TPU v7x, 256 devices: a whole 4x4x8 slice. The times are simulated.
256 devices in a mesh: seq: 16 (over y, z_hi, core), mp: 16 (over z_lo, x).
Axes of the slice: x: 4, y: 4, z: 8 (z_hi: 2, z_lo: 4; z = z_hi * 4 + z_lo), core: 2. Of those that a mesh axis runs over, the one named last changes fastest.
Arguments:
- hidden_in: bfloat16 [2048, 2048], P('seq'), may hold values from -0.59765625 to 0.59765625
- input_gain: float32 [2048], replicated, may hold values from 0.25 to 1.75
- w_query: bfloat16 [2048, 2048], P(None, 'mp'), may hold values from -0.125 to 0.125
- key_value_weight: bfloat16 [2048, 4096], P(None, 'mp'), may hold values from -1 to 1, as said below
- query_gain: float32 [128], replicated, may hold values from 0.25 to 1.75
- key_gain: float32 [128], replicated, may hold values from 0.25 to 1.75
- w_out: bfloat16 [2048, 2048], P('mp'), may hold values from -0.125 to 0.125
- post_gain: float32 [2048], replicated, may hold values from 0.25 to 1.75
- w_gate: bfloat16 [2048, 6144], P(None, 'mp'), may hold values from -0.125 to 0.125
- w_up: bfloat16 [2048, 6144], P(None, 'mp'), may hold values from -0.125 to 0.125
- w_down: bfloat16 [6144, 2048], P('mp'), may hold values from -0.078125 to 0.078125
- prefix_slot_cache: bfloat16 [32, 256, 8, 256], P('seq'), may hold values from -240 to 240, as said below
- block_table: int32 [32], replicated, may hold values from 0 to 31, each once
- request_prefix: int32 [32], replicated, may hold values from 0 to 3
- suffix_lengths: int32 [32], replicated, may hold values from 1 to 256, 2048 in all
Outputs:
- hidden_out: bfloat16 [2048, 2048], P('seq', 'mp')
- suffix_key_values: bfloat16 [2048, 2048], P('seq', 'mp')
Inputs may be any that keep to these rules, and one draw needn't show every extreme that they name: block_table[p * 8 + i] is the slot holding block i of prefix p; every slot appears once. `suffix_lengths`: the lengths add up to 2048 and the longest is exactly 256. `prefix_slot_cache`: per slot, position and key-value head: a key in the first 128 entries, a value in the last 128. `key_value_weight`: columns of key-value head k: 2 equal blocks of 256, starting at k * 2 * 2 * 128.
All inputs are finite; a program needn't handle non-finite values.
Results may differ from a plain program's by a relative error of at most 0.025.
The roundings to bfloat16 on the way count: a program that leaves them out, or rounds other values in their place, can miss the bound.
Values may be sent and summed in bfloat16 or wider, within the bound.
A program may use at most 64 MiB of HBM per device.

v0:
```python
import math

import jax
import jax.numpy as jnp
from jax import lax
from jax.sharding import PartitionSpec as P

QUERY_HEADS = 16
KEY_VALUE_HEADS = 8
HEAD_WIDTH = 128
N_PREFIX = 4


EPSILON = 1e-06
THETA = 1000000.0
NEGATIVE_FLOOR = -1e30


def token_tables(request_prefix, suffix_lengths, positions, prefix_length):
    request_ends = jnp.cumsum(suffix_lengths)
    starts = request_ends - suffix_lengths
    inside = (
        (positions[:, None] >= starts[None, :]) & (positions[:, None] < request_ends[None, :])
    ).astype(jnp.int32)
    request_ids = jnp.arange(suffix_lengths.shape[0], dtype=jnp.int32)
    request_of = jnp.sum(inside * request_ids[None, :], axis=1)
    start_of = jnp.sum(inside * starts[None, :], axis=1)
    prefix_of = jnp.sum(inside * request_prefix[None, :], axis=1)
    rotary_pos = prefix_length + positions - start_of
    return (request_of, prefix_of, rotary_pos)


def row_norm(values, gain):
    return values * lax.rsqrt(jnp.mean(values * values, axis=-1, keepdims=True) + EPSILON) * gain


def head_norm(values, gain):
    return values * lax.rsqrt(jnp.mean(values * values, axis=-1, keepdims=True) + EPSILON) * gain


def rotate(values, rotary_pos):
    half_dim = values.shape[-1] // 2
    freq_ids = jnp.arange(half_dim).astype(jnp.float32)
    inverse = jnp.exp(freq_ids * (-2.0 * math.log(THETA) / values.shape[-1]))
    angles = rotary_pos.astype(jnp.float32)[:, None] * inverse[None, :]
    cosine = jnp.cos(angles)[:, None, :]
    sine_part = jnp.sin(angles)[:, None, :]
    first_half = values[..., :half_dim]
    second_half = values[..., half_dim:]
    return jnp.concatenate(
        [
            first_half * cosine - second_half * sine_part,
            second_half * cosine + first_half * sine_part,
        ],
        axis=-1,
    )


def allowed_keys(query_req, query_pre, query_pos, key_pre, key_req, key_pos):
    same_prefix = key_pre[None, :] == query_pre[:, None]
    same_request = (key_req[None, :] == query_req[:, None]) & (
        key_pos[None, :] <= query_pos[:, None]
    )
    return same_prefix | same_request


def group_partial(query_rows_all, allowed, key_row_block, value_row_block):
    scaling = 1.0 / math.sqrt(query_rows_all.shape[-1])
    scores = (
        jnp.einsum(
            "nkgd,mkd->nkgm", query_rows_all, key_row_block, preferred_element_type=jnp.float32
        )
        * scaling
    )
    allowed_full = allowed[:, None, None, :]
    scores = jnp.where(allowed_full, scores, NEGATIVE_FLOOR)
    highest_score = jnp.max(scores, axis=-1)
    weights = jnp.where(allowed_full, jnp.exp(scores - highest_score[..., None]), 0.0)
    total_weight = jnp.sum(weights, axis=-1)
    rounded = weights.astype(jnp.bfloat16)
    summed = jnp.einsum(
        "nkgm,mkd->nkgd", rounded, value_row_block, preferred_element_type=jnp.float32
    )
    layer_output = (summed / jnp.maximum(total_weight, 1.0)[..., None]).astype(jnp.bfloat16)
    return (highest_score, total_weight, layer_output)


def tile_partials(query_rows, query_req, query_pre, query_pos, bundle, tile_rows):
    key_row_block, value_row_block, key_pre, key_req, key_pos = bundle
    token_count = query_rows.shape[0]
    tile_count = token_count // tile_rows
    shaped = (
        query_rows.reshape((tile_count, tile_rows) + query_rows.shape[1:]),
        query_req.reshape(tile_count, tile_rows),
        query_pre.reshape(tile_count, tile_rows),
        query_pos.reshape(tile_count, tile_rows),
    )

    def one_tile(members):
        tile_queries, tile_req, tile_pre, tile_pos = members
        allowed = allowed_keys(tile_req, tile_pre, tile_pos, key_pre, key_req, key_pos)

        def computed(unused):
            return group_partial(tile_queries, allowed, key_row_block, value_row_block)

        def skipped(unused):
            stats_shape = tile_queries.shape[:-1]
            return (
                jnp.full(stats_shape, NEGATIVE_FLOOR, jnp.float32),
                jnp.zeros(stats_shape, jnp.float32),
                jnp.zeros(tile_queries.shape, jnp.bfloat16),
            )

        return lax.cond(jnp.any(allowed), computed, skipped, 0)

    highest_score, total_weight, layer_output = lax.map(one_tile, shaped)
    stats_shape = (token_count,) + query_rows.shape[1:-1]
    return (
        highest_score.reshape(stats_shape),
        total_weight.reshape(stats_shape),
        layer_output.reshape(query_rows.shape),
    )


def local(
    hidden_in,
    input_gain,
    w_query,
    key_value_weight,
    query_gain,
    key_gain,
    w_out,
    post_gain,
    w_gate,
    w_up,
    w_down,
    prefix_slot_cache,
    block_table,
    request_prefix,
    suffix_lengths,
):
    seq_count = lax.axis_size("seq")
    model_count = lax.axis_size("mp")
    my_seq = lax.axis_index("seq")
    my_model = lax.axis_index("mp")
    rows_here = hidden_in.shape[0]
    local_heads = w_query.shape[1] // HEAD_WIDTH
    group_width = QUERY_HEADS // KEY_VALUE_HEADS
    shared_heads = max(1, local_heads // group_width)
    query_per_head = local_heads // shared_heads
    pair_width = 2 * HEAD_WIDTH
    first_shared = my_model * local_heads // group_width
    blocks_here = prefix_slot_cache.shape[0]
    block_rows = prefix_slot_cache.shape[1]
    cache_extent = blocks_here * block_rows
    slot_total = blocks_here * seq_count
    prefix_length = slot_total // N_PREFIX * block_rows
    all_tokens = rows_here * seq_count
    hidden_f32 = hidden_in.astype(jnp.float32)
    normed = row_norm(hidden_f32, input_gain).astype(jnp.bfloat16)
    own_pos = my_seq * rows_here + jnp.arange(rows_here, dtype=jnp.int32)
    own_req, own_pre, own_rot = token_tables(request_prefix, suffix_lengths, own_pos, prefix_length)
    query_raw = jnp.dot(normed, w_query, preferred_element_type=jnp.float32).reshape(
        rows_here, local_heads, HEAD_WIDTH
    )
    query_rows_all = rotate(head_norm(query_raw, query_gain), own_rot).astype(jnp.bfloat16)
    pair_block = jnp.dot(normed, key_value_weight, preferred_element_type=jnp.float32).astype(
        jnp.bfloat16
    )
    share_ratio = max(1, group_width // local_heads)
    pair_split = pair_block.reshape(rows_here, shared_heads, 2, HEAD_WIDTH)
    key_row_block = rotate(
        head_norm(pair_split[:, :, 0].astype(jnp.float32), key_gain), own_rot
    ).astype(jnp.bfloat16)
    pairs_mine = jnp.stack([key_row_block, pair_split[:, :, 1]], axis=2).reshape(
        rows_here, shared_heads, pair_width
    )
    cache_cols = shared_heads * pair_width // share_ratio
    suffix_key_values = lax.dynamic_slice_in_dim(
        pairs_mine.reshape(rows_here, shared_heads * pair_width),
        my_model % share_ratio * cache_cols,
        cache_cols,
        1,
    )
    slot_ids = jnp.arange(slot_total, dtype=jnp.int32)
    owner_hits = (block_table[:, None] == slot_ids[None, :]).astype(jnp.int32)
    slot_prefix = jnp.sum(owner_hits * (slot_ids // (slot_total // N_PREFIX))[:, None], axis=0)
    cache_mine = lax.dynamic_slice_in_dim(prefix_slot_cache, first_shared, shared_heads, 2).reshape(
        cache_extent, shared_heads, pair_width
    )
    query_all = lax.all_gather(
        query_rows_all.reshape(rows_here, local_heads * HEAD_WIDTH), "seq", axis=0, tiled=True
    )
    query_all = query_all.reshape(all_tokens, shared_heads, query_per_head, HEAD_WIDTH)
    all_pos = jnp.arange(all_tokens, dtype=jnp.int32)
    all_req, all_pre, _ = token_tables(request_prefix, suffix_lengths, all_pos, prefix_length)
    group_pre = jnp.repeat(
        lax.dynamic_slice_in_dim(slot_prefix, my_seq * blocks_here, blocks_here), block_rows
    )
    key_positions = my_seq * rows_here + jnp.arange(rows_here, dtype=jnp.int32)
    group_req, _, _ = token_tables(request_prefix, suffix_lengths, key_positions, prefix_length)
    all_keys = jnp.concatenate([cache_mine[..., :HEAD_WIDTH], pairs_mine[..., :HEAD_WIDTH]], axis=0)
    all_values = jnp.concatenate(
        [cache_mine[..., HEAD_WIDTH:], pairs_mine[..., HEAD_WIDTH:]], axis=0
    )
    key_pre = jnp.concatenate([group_pre, jnp.full((rows_here,), -1, jnp.int32)])
    key_req = jnp.concatenate([jnp.full((cache_extent,), -1, jnp.int32), group_req])
    key_pos = jnp.concatenate([jnp.zeros((cache_extent,), jnp.int32), key_positions])
    bundle = (all_keys, all_values, key_pre, key_req, key_pos)
    highest_score, total_weight, layer_output = tile_partials(
        query_all, all_req, all_pre, all_pos, bundle, min(512, all_tokens)
    )
    highest_score = highest_score.reshape(seq_count, rows_here, shared_heads, query_per_head)
    total_weight = total_weight.reshape(seq_count, rows_here, shared_heads, query_per_head)
    layer_output = layer_output.reshape(
        seq_count, rows_here, shared_heads, query_per_head, HEAD_WIDTH
    )
    widened = lax.optimization_barrier(layer_output).astype(jnp.float32)
    result_back, peak_back, total_back = (
        lax.all_to_all(widened, "seq", split_axis=0, concat_axis=0, tiled=True),
        lax.all_to_all(highest_score, "seq", split_axis=0, concat_axis=0, tiled=True),
        lax.all_to_all(total_weight, "seq", split_axis=0, concat_axis=0, tiled=True),
    )
    best_score = jnp.max(peak_back, axis=0)
    scaling = total_back * jnp.exp(peak_back - best_score[None])
    attended = (
        jnp.sum(scaling[..., None] * result_back, axis=0) / jnp.sum(scaling, axis=0)[..., None]
    )
    attended = attended.astype(jnp.bfloat16).reshape(rows_here, local_heads * HEAD_WIDTH)
    partial_out = jnp.dot(attended, w_out, preferred_element_type=jnp.float32)
    column_count = hidden_in.shape[1] // model_count
    summed = lax.psum(partial_out.astype(jnp.bfloat16), "mp").astype(jnp.float32)
    residual = (hidden_f32 + summed).astype(jnp.bfloat16)
    residual_cols = lax.dynamic_slice_in_dim(residual, my_model * column_count, column_count, 1)
    post_normed = row_norm(residual.astype(jnp.float32), post_gain).astype(jnp.bfloat16)
    gate_terms = jnp.dot(post_normed, w_gate, preferred_element_type=jnp.float32)
    up_terms = jnp.dot(post_normed, w_up, preferred_element_type=jnp.float32)
    middle = (jax.nn.silu(gate_terms) * up_terms).astype(jnp.bfloat16)
    down_terms = jnp.dot(middle, w_down, preferred_element_type=jnp.float32)
    hidden_part = lax.psum_scatter(
        down_terms.astype(jnp.bfloat16), "mp", scatter_dimension=1, tiled=True
    ).astype(jnp.float32)
    hidden_out = (residual_cols.astype(jnp.float32) + hidden_part).astype(jnp.bfloat16)
    return (hidden_out, suffix_key_values)


def solution(mesh):
    in_specs = (
        P("seq", None),
        P(),
        P(None, "mp"),
        P(None, "mp"),
        P(),
        P(),
        P("mp", None),
        P(),
        P(None, "mp"),
        P(None, "mp"),
        P("mp", None),
        P("seq", None, None, None),
        P(),
        P(),
        P(),
    )
    out_specs = (P("seq", "mp"), P("seq", "mp"))
    return jax.shard_map(local, mesh=mesh, in_specs=in_specs, out_specs=out_specs, check_vma=False)
```

profile of v0, /device:TPU:8, one launch (start us, length us, event | category | flops | bytes accessed | tf_op | source)
XLA Modules:
  0.0 402.8 jit_solution(13331135312913714287)
XLA Ops:
  7.3 1.4 fusion.20
  8.7 1.8 convolution_convert_fusion.2
  12.8 33.7 %all_gather.3 = bf16[2048,128]{0,1:T(8,128)(2,1)S(1)} all-gather(bf16[128,128]{0,1:T(8,128)(2,1)S(1)} %pad_maximum_fusion.3), channel_id=1, replica_groups=mesh['seq'=16,'mp'=16] {'seq'}, dimensions={0}, use_global_device_ids=true | all-gather | bytes 557056 | tf_op jit(solution)/shard_map/all_gather | solution.py:191
  47.5 33.2 %while.14 = (s32[]{:T(128)}, f32[4,512,1,1]{1,3,2,0:T(1,128)S(1)}, f32[4,512,1,1]{1,3,2,0:T(1,128)}, bf16[4,512,1,1,128]{4,1,3,2,0:T(8,128)(2,1)}, s32[640]{0:T(...) while((s32[]{:T(128)}, f32[4,512,1,1]{1,3,2,0:T(1,128)S(1)}, ...), condition=%wide.region_15.16_spmd, body=%wide.region_9.15_spmd.sunk | while | flops 172817920 | bytes 6144739 | solution.py:116
  47.5 1.0 fusion.76
  49.2 4.6 %conditional.2 = (f32[1,512,1,1]{1,3,2,0:T(1,128)}, f32[1,512,1,1]{1,3,2,0:T(1,128)}, bf16[1,512,1,1,128]{4,1,3,2,0:T(8,128)(2,1)S(1)}) conditional(s32[]{:T(128)} %convert_element_type.195, () %tuple.64, (pred[512,640]{1,0:T(32,128)(4,1)S(1)}, bf16[4,512,1,1,128]{4,1,3,2,0:T(8,128)(2,1)S(1)}, s32[]{:T(128)}, bf16[640,1,128]{2,0,1:T(8,128)(2,1)S(1)}, ...), branch_computations={%region_11.11_spmd, %region_12.14_spmd} | conditional | flops 170851840 | bytes 5519388 | solution.py:114
  49.2 1.1 fusion.66
  50.3 1.7 fusion.5
  52.0 0.7 broadcast_maximum_fusion
  52.7 1.1 fusion.3
  53.8 1.3 constant_dynamic-update-slice_fusion.5
  55.8 1.0 fusion.76
  57.5 4.6 %conditional.2 = (f32[1,512,1,1]{1,3,2,0:T(1,128)}, f32[1,512,1,1]{1,3,2,0:T(1,128)}, bf16[1,512,1,1,128]{4,1,3,2,0:T(8,128)(2,1)S(1)}) conditional(s32[]{:T(128)} %convert_element_type.195, () %tuple.64, (pred[512,640]{1,0:T(32,128)(4,1)S(1)}, bf16[4,512,1,1,128]{4,1,3,2,0:T(8,128)(2,1)S(1)}, s32[]{:T(128)}, bf16[640,1,128]{2,0,1:T(8,128)(2,1)S(1)}, ...), branch_computations={%region_11.11_spmd, %region_12.14_spmd} | conditional | flops 170851840 | bytes 5519388 | solution.py:114
  57.5 1.1 fusion.66
  58.6 1.7 fusion.5
  60.3 0.7 broadcast_maximum_fusion
  61.0 1.1 fusion.3
  62.1 1.3 constant_dynamic-update-slice_fusion.5
  64.1 1.0 fusion.76
  65.8 4.6 %conditional.2 = (f32[1,512,1,1]{1,3,2,0:T(1,128)}, f32[1,512,1,1]{1,3,2,0:T(1,128)}, bf16[1,512,1,1,128]{4,1,3,2,0:T(8,128)(2,1)S(1)}) conditional(s32[]{:T(128)} %convert_element_type.195, () %tuple.64, (pred[512,640]{1,0:T(32,128)(4,1)S(1)}, bf16[4,512,1,1,128]{4,1,3,2,0:T(8,128)(2,1)S(1)}, s32[]{:T(128)}, bf16[640,1,128]{2,0,1:T(8,128)(2,1)S(1)}, ...), branch_computations={%region_11.11_spmd, %region_12.14_spmd} | conditional | flops 170851840 | bytes 5519388 | solution.py:114
  65.8 1.1 fusion.66
  66.9 1.7 fusion.5
  68.6 0.7 broadcast_maximum_fusion
  69.3 1.1 fusion.3
  70.4 1.3 constant_dynamic-update-slice_fusion.5
  72.4 1.0 fusion.76
  74.1 4.6 %conditional.2 = (f32[1,512,1,1]{1,3,2,0:T(1,128)}, f32[1,512,1,1]{1,3,2,0:T(1,128)}, bf16[1,512,1,1,128]{4,1,3,2,0:T(8,128)(2,1)S(1)}) conditional(s32[]{:T(128)} %convert_element_type.195, () %tuple.64, (pred[512,640]{1,0:T(32,128)(4,1)S(1)}, bf16[4,512,1,1,128]{4,1,3,2,0:T(8,128)(2,1)S(1)}, s32[]{:T(128)}, bf16[640,1,128]{2,0,1:T(8,128)(2,1)S(1)}, ...), branch_computations={%region_11.11_spmd, %region_12.14_spmd} | conditional | flops 170851840 | bytes 5519388 | solution.py:114
  74.1 1.1 fusion.66
  75.1 1.7 fusion.5
  76.9 0.7 broadcast_maximum_fusion
  77.6 1.1 fusion.3
  78.7 1.3 constant_dynamic-update-slice_fusion.5
  80.0 0.7 constant_dynamic-update-slice_fusion.6
  80.6 13.7 %all_to_all.15 = f32[16,128,1,1]{1,3,2,0:T(1,128)S(1)} all-to-all(f32[16,128,1,1]{1,3,2,0:T(1,128)S(1)} %bitcast.115), channel_id=1, replica_groups=mesh['seq'=16,'mp'=16] {'seq'}, dimensions={0} | all-to-all | bytes 16384 | tf_op jit(solution)/shard_map/all_to_all | solution.py:221
  94.3 4.7 %all-to-all-start = ((f32[16,128,1,1]{1,3,2,0:T(1,128)}), f32[16,128,1,1]{1,3,2,0:T(1,128)S(1)}, u32[]{:S(2)}, u32[]{:S(2)}) async-start(f32[16,128,1,1]{1,3,2,0:T(1,128)} %bitcast.29), calls=%async_computation | async-start | bytes 16384 | tf_op jit(solution)/shard_map/all_to_all | solution.py:222
  99.0 2.1 convert_element_type.121
  101.2 6.5 %all-to-all-done = f32[16,128,1,1]{1,3,2,0:T(1,128)S(1)} async-done(((f32[16,128,1,1]{1,3,2,0:T(1,128)}), f32[16,128,1,1]{1,3,2,0:T(1,128)S(1)}, u32[]{:S(2)}, u32[]{:S(2)}) %all-to-all-start) | async-done | bytes 8224 | tf_op jit(solution)/shard_map/all_to_all | solution.py:222
  107.6 4.9 %all-to-all-start.2 = ((f32[16,128,1,1,128]{4,1,3,2,0:T(8,128)}), f32[16,128,1,1,128]{4,1,3,2,0:T(8,128)S(1)}, u32[]{:S(2)}, u32[]{:S(2)}) async-start(f32[16,128,1,1,128]{4,1,3,2,0:T(8,128)} %convert_element_type.121), calls=%async_computation.2 | async-start | bytes 2097152 | tf_op jit(solution)/shard_map/all_to_all | solution.py:220
  112.6 23.0 %all-to-all-done.2 = f32[16,128,1,1,128]{4,1,3,2,0:T(8,128)S(1)} async-done(((f32[16,128,1,1,128]{4,1,3,2,0:T(8,128)}), f32[16,128,1,1,128]{4,1,3,2,0:T(8,128)S(1)}, u32[]{:S(2)}, u32[]{:S(2)}) %all-to-all-start.2) | async-done | bytes 1048608 | tf_op jit(solution)/shard_map/all_to_all | solution.py:220
  136.0 0.7 copy-done.3
  136.7 1.2 convolution_convert_fusion.1
  137.9 167.1 %all-reduce.5.cloned.1.call-done = bf16[128,2048]{1,0:T(8,128)(2,1)} async-done(((bf16[128,2048]{1,0:T(8,128)(2,1)}), bf16[128,2048]{1,0:T(8,128)(2,1)}) %all-reduce.5.cloned.1.call-update) | async-done | bytes 524304 | tf_op jit(solution)/shard_map/psum | solution.py:232
  305.0 1.4 fusion.17
  307.0 2.8 convolution_convert_fusion
  309.8 1.0 copy.55
  310.9 0.7 copy.60
  311.6 82.8 %reduce-scatter.4.cloned.1.call-done = bf16[128,128]{1,0:T(8,128)(2,1)} async-done(((bf16[2048,128]{1,0:T(8,128)(2,1)}), bf16[128,128]{1,0:T(8,128)(2,1)}) %reduce-scatter.4.cloned.1.call-update) | async-done | bytes 32784
  394.4 0.9 copy.56
  (94 shorter events, 6.9 us)
Async XLA Ops:
  7.2 39.6 %copy-start = (bf16[2,256,8,256]{3,2,1,0:T(8,128)(2,1)S(1)}, bf16[2,256,8,256]{3,2,1,0:T(8,128)(2,1)}, u32[]{:S(2)}) copy-start(bf16[2,256,8,256]{3,2,1,0:T(8,128)(2,1)} %param.30) | copy-start | bytes 6291460
  7.2 3.5 copy-start.12
  7.3 3.7 copy-start.6
  7.3 4.1 %copy-start.7 = (s32[32]{0:T(128)S(1)}, s32[32]{0:T(128)}, u32[]{:S(2)}) copy-start(s32[32]{0:T(128)} %param.32) | copy-start | bytes 388
  7.3 4.4 %copy-start.1 = (bf16[128,2048]{1,0:T(8,128)(2,1)S(1)}, bf16[128,2048]{1,0:T(8,128)(2,1)}, u32[]{:S(2)}) copy-start(bf16[128,2048]{1,0:T(8,128)(2,1)} %param.19) | copy-start | bytes 1572868
  7.3 4.4 %copy-start.9 = (bf16[2048,128]{1,0:T(8,128)(2,1)S(1)}, bf16[2048,128]{1,0:T(8,128)(2,1)}, u32[]{:S(2)}) copy-start(bf16[2048,128]{1,0:T(8,128)(2,1)} %param.21) | copy-start | bytes 1572868
  7.3 4.4 %copy-start.10 = (f32[2048]{0:T(1024)S(1)}, f32[2048]{0:T(1024)}, u32[]{:S(2)}) copy-start(f32[2048]{0:T(1024)} %param.20) | copy-start | bytes 24580
  10.5 1.6 copy-start.4
  10.5 1.7 copy-start.5
  94.3 13.3 %all-to-all-start = ((f32[16,128,1,1]{1,3,2,0:T(1,128)}), f32[16,128,1,1]{1,3,2,0:T(1,128)S(1)}, u32[]{:S(2)}, u32[]{:S(2)}) async-start(f32[16,128,1,1]{1,3,2,0:T(1,128)} %bitcast.29), calls=%async_computation | async-start | bytes 16384 | tf_op jit(solution)/shard_map/all_to_all | solution.py:222
  107.6 28.0 %all-to-all-start.2 = ((f32[16,128,1,1,128]{4,1,3,2,0:T(8,128)}), f32[16,128,1,1,128]{4,1,3,2,0:T(8,128)S(1)}, u32[]{:S(2)}, u32[]{:S(2)}) async-start(f32[16,128,1,1,128]{4,1,3,2,0:T(8,128)} %convert_element_type.121), calls=%async_computation.2 | async-start | bytes 2097152 | tf_op jit(solution)/shard_map/all_to_all | solution.py:220
  112.5 192.5 %all-reduce.5.cloned.1.call-start = ((), (), s32[]{:S(2)}) async-start(), calls=%async_computation.4 | async-start | bytes 1048576 | tf_op jit(solution)/shard_map/psum | solution.py:232
  135.6 1.0 copy-start.3
  136.0 169.0 %copy-start.2 = (bf16[128,2048]{1,0:T(8,128)(2,1)S(1)}, bf16[128,2048]{1,0:T(8,128)(2,1)}, u32[]{:S(2)}) copy-start(bf16[128,2048]{1,0:T(8,128)(2,1)} %param.19) | copy-start | bytes 1572868
  137.8 168.6 %copy-start.11 = (f32[2048]{0:T(1024)S(1)}, f32[2048]{0:T(1024)}, u32[]{:S(2)}) copy-start(f32[2048]{0:T(1024)} %param.26) | copy-start | bytes 24580
  137.9 256.6 %reduce-scatter.4.cloned.1.call-start = ((), (), s32[]{:S(2)}) async-start(), calls=%async_computation.5 | async-start | bytes 557056
  305.0 1.6 copy-start.8
Sparse Core Ops, SparseCore 0:
  138.0 166.9 all-reduce.4
  311.0 83.4 reduce-scatter.3
where the time goes:
time: 404 us; the launch traced here: 403 us
  waiting for transfers between devices  279 us (69%)
  blocking collectives  47.4 us (12%)
  other arithmetic  20.9 us (5%)
  matrix products  15.3 us (4%)
  between operations  14.5 us (4%)
  local copies, waits for them, and re-layouts  12.8 us (3%)
  starting transfers between devices  9.69 us (2%)
    psum x1, waiting for transfers between devices, local(): lax.psum(partial_out.astype(jnp.bfloat16), 'mp').astype(jnp.float32)  167 us
    unnamed x3, waiting for transfers between devices  82.9 us
    all_gather x1, blocking collectives, local(): lax.all_gather(query_rows_all.reshape(rows_here, local_heads * HEAD_WIDTH...  33.7 us
    all_to_all x1, waiting for transfers between devices, local(): lax.all_to_all(widened, 'seq', split_axis=0, concat_axis=0, tiled=True)  23 us
    all_to_all x1, blocking collectives, local(): lax.all_to_all(highest_score, 'seq', split_axis=0, concat_axis=0, tiled=T...  13.7 us
  transfers between devices with their start and end apart: 4, of which 4 were waited for; matrix products, arithmetic and copies ran while one was open for 1% of the time, Pallas kernels for 0%

commit v1 on v0

v1 whole, which is shorter than its diff:
```python
import functools
import math

import jax
import jax.numpy as jnp
from jax import lax
from jax.experimental import pallas as pl
from jax.experimental.pallas import tpu as pltpu
from jax.sharding import PartitionSpec as P

HEAD = 128
N_PREFIX = 4
EPSILON = 1e-06
THETA = 1000000.0
FLOOR = -1e30
MESH = pl.DeviceIdType.MESH
F32 = jnp.float32
BF16 = jnp.bfloat16


def push(src, dst, send_sem, recv_sem, axis, peer):
    return pltpu.make_async_remote_copy(
        src_ref=src,
        dst_ref=dst,
        send_sem=send_sem,
        recv_sem=recv_sem,
        device_id={axis: peer},
        device_id_type=MESH,
    )


def greet(axis, count, me):
    barrier = pltpu.get_barrier_semaphore()

    def one(step, carry):
        pl.semaphore_signal(
            barrier, inc=1, device_id={axis: lax.rem(me + step, count)}, device_id_type=MESH
        )
        return carry

    lax.fori_loop(1, count, one, 0)
    return barrier


def normalize(values, gain):
    return values * lax.rsqrt(jnp.mean(values * values, axis=-1, keepdims=True) + EPSILON) * gain


def attn_kernel(
    count,
    hidden_ref,
    gain_ref,
    wq_ref,
    wkv_ref,
    qgain_ref,
    kgain_ref,
    cos_ref,
    sin_ref,
    cache_ref,
    table_ref,
    prefix_ref,
    length_ref,
    att_ref,
    skv_ref,
    q_all,
    keys,
    values_t,
    out_send,
    stat_send,
    out_recv,
    stat_recv,
    q_send_sem,
    q_recv_sem,
    o_send_sem,
    o_recv_sem,
    s_send_sem,
    s_recv_sem,
):
    me = lax.axis_index("seq")
    my_model = lax.axis_index("mp")
    rows = hidden_ref.shape[0]
    cached = cache_ref.shape[0]
    slot_rows = cached // 2
    barrier = greet("seq", count, me)

    normed = normalize(hidden_ref[...].astype(F32), gain_ref[...]).astype(BF16)
    cosine, sine = cos_ref[...], sin_ref[...]

    def rope(x):
        return x * cosine + pltpu.roll(x, HEAD // 2, 1) * sine

    q_raw = jnp.dot(normed, wq_ref[...], preferred_element_type=F32)
    q_all[me] = rope(normalize(q_raw, qgain_ref[...])).astype(BF16)
    pl.semaphore_wait(barrier, count - 1)

    def send_q(step, carry):
        peer = lax.rem(me + step, count)
        push(
            q_all.at[me], q_all.at[me], q_send_sem.at[peer], q_recv_sem.at[me], "seq", peer
        ).start()
        return carry

    lax.fori_loop(1, count, send_q, 0)

    pair = jnp.dot(normed, wkv_ref[...], preferred_element_type=F32).astype(BF16)
    key = rope(normalize(pair[:, :HEAD].astype(F32), kgain_ref[...])).astype(BF16)
    value = pair[:, HEAD:]
    skv_ref[...] = jnp.where(lax.rem(my_model, 2) == 0, key.astype(F32), value.astype(F32)).astype(
        BF16
    )
    keys[pl.ds(0, cached), :] = cache_ref[:, :HEAD]
    keys[pl.ds(cached, rows), :] = key
    values_t[:, pl.ds(0, cached)] = cache_ref[:, HEAD:].astype(F32).T.astype(BF16)
    values_t[:, pl.ds(cached, rows)] = value.astype(F32).T.astype(BF16)

    requests = length_ref.shape[1]
    lengths = jnp.broadcast_to(length_ref[...], (requests, requests))
    row_id = lax.broadcasted_iota(jnp.int32, (requests, requests), 0)
    col_id = lax.broadcasted_iota(jnp.int32, (requests, requests), 1)
    ends = jnp.sum(jnp.where(col_id <= row_id, lengths, 0), axis=1, keepdims=True)
    starts = jnp.sum(jnp.where(col_id < row_id, lengths, 0), axis=1, keepdims=True)
    prefixes = prefix_ref[...]
    table = table_ref[...]
    slots = table.shape[1]
    owner = lax.broadcasted_iota(jnp.int32, (1, slots), 1) // (slots // N_PREFIX)
    slot_a = jnp.sum(jnp.where(table == 2 * me, owner, 0), axis=1, keepdims=True)
    slot_b = jnp.sum(jnp.where(table == 2 * me + 1, owner, 0), axis=1, keepdims=True)
    scale = 1.0 / math.sqrt(HEAD)

    def partial(chunk):
        position = chunk * rows + lax.broadcasted_iota(jnp.int32, (1, rows), 1)
        inside = (position >= starts) & (position < ends)
        start_of = jnp.sum(jnp.where(inside, starts, 0), axis=0, keepdims=True)
        prefix_of = jnp.sum(jnp.where(inside, prefixes, 0), axis=0, keepdims=True)
        score = (
            lax.dot_general(
                keys[...], q_all[chunk], (((1,), (1,)), ((), ())), preferred_element_type=F32
            )
            * scale
        )
        key_pos = me * rows + lax.broadcasted_iota(jnp.int32, (rows, rows), 0)
        score_a = jnp.where(prefix_of == slot_a, score[:slot_rows], FLOOR)
        score_b = jnp.where(prefix_of == slot_b, score[slot_rows:cached], FLOOR)
        score_c = jnp.where((key_pos >= start_of) & (key_pos <= position), score[cached:], FLOOR)
        score = jnp.concatenate([score_a, score_b, score_c], axis=0)
        peak = jnp.max(score, axis=0, keepdims=True)
        weight = jnp.exp(score - jnp.where(peak < 0.1 * FLOOR, 0.0, peak))
        total = jnp.sum(weight, axis=0, keepdims=True)
        out = jnp.dot(values_t[...], weight.astype(BF16), preferred_element_type=F32)
        out = (out / jnp.maximum(total, 1.0)).astype(BF16)
        stats = jnp.concatenate(
            [jnp.broadcast_to(peak, (4, rows)), jnp.broadcast_to(total, (4, rows))], axis=0
        )
        return out, stats

    own_out, own_stats = partial(me)
    out_recv[me] = own_out
    stat_recv[me] = own_stats

    def answer(step, carry):
        peer = lax.rem(me + count - step, count)
        push(
            q_all.at[peer], q_all.at[peer], q_send_sem.at[peer], q_recv_sem.at[peer], "seq", peer
        ).wait_recv()
        out, stats = partial(peer)
        out_send[peer] = out
        stat_send[peer] = stats
        push(
            out_send.at[peer], out_recv.at[me], o_send_sem.at[peer], o_recv_sem.at[me], "seq", peer
        ).start()
        push(
            stat_send.at[peer],
            stat_recv.at[me],
            s_send_sem.at[peer],
            s_recv_sem.at[me],
            "seq",
            peer,
        ).start()
        return carry

    lax.fori_loop(1, count, answer, 0)

    def collect(step, carry):
        peer = lax.rem(me + step, count)
        push(
            out_send.at[peer], out_recv.at[peer], o_send_sem.at[peer], o_recv_sem.at[peer], "seq", peer
        ).wait()
        push(
            stat_send.at[peer],
            stat_recv.at[peer],
            s_send_sem.at[peer],
            s_recv_sem.at[peer],
            "seq",
            peer,
        ).wait()
        push(
            q_all.at[me], q_all.at[me], q_send_sem.at[peer], q_recv_sem.at[peer], "seq", peer
        ).wait_send()
        return carry

    lax.fori_loop(1, count, collect, 0)
    best = stat_recv[0, 0:1, :]
    for group in range(1, count):
        best = jnp.maximum(best, stat_recv[group, 0:1, :])
    below = jnp.zeros((1, rows), F32)
    above = jnp.zeros((HEAD, rows), F32)
    for group in range(count):
        factor = stat_recv[group, 4:5, :] * jnp.exp(stat_recv[group, 0:1, :] - best)
        below += factor
        above += factor * out_recv[group].astype(F32)
    att_ref[...] = (above / below).T.astype(BF16)


def ffn_kernel(
    count,
    att_ref,
    hidden_ref,
    wo_ref,
    gain_ref,
    wg_hbm,
    wu_hbm,
    wd_hbm,
    out_ref,
    wg,
    wu,
    wd,
    part_send,
    part_recv,
    residual,
    post,
    down_send,
    down_recv,
    w_sem,
    a_send_sem,
    a_recv_sem,
    r_send_sem,
    r_recv_sem,
    d_send_sem,
    d_recv_sem,
):
    me = lax.axis_index("mp")
    barrier = greet("mp", count, me)
    loads = [
        pltpu.make_async_copy(wg_hbm, wg, w_sem.at[0]),
        pltpu.make_async_copy(wu_hbm, wu, w_sem.at[1]),
        pltpu.make_async_copy(wd_hbm, wd, w_sem.at[2]),
    ]
    for load in loads:
        load.start()
    width = HEAD

    def columns(chunk):
        return pl.ds(pl.multiple_of(chunk * width, width), width)

    att = att_ref[...]
    pl.semaphore_wait(barrier, count - 1)

    def send_part(step, carry):
        peer = lax.rem(me + step, count)
        part_send[peer] = jnp.dot(
            att, wo_ref[:, columns(peer)], preferred_element_type=F32
        ).astype(BF16)
        push(
            part_send.at[peer], part_recv.at[me], a_send_sem.at[peer], a_recv_sem.at[me], "mp", peer
        ).start()
        return carry

    lax.fori_loop(1, count, send_part, 0)
    mine = jnp.dot(att, wo_ref[:, columns(me)], preferred_element_type=F32)

    def add_part(step, total):
        peer = lax.rem(me + count - step, count)
        push(
            part_send.at[peer], part_recv.at[peer], a_send_sem.at[peer], a_recv_sem.at[peer], "mp", peer
        ).wait()
        return total + part_recv[peer].astype(F32)

    mine = lax.fori_loop(1, count, add_part, mine)
    residual[me] = (hidden_ref[:, columns(me)].astype(F32) + mine).astype(BF16)

    def send_residual(step, carry):
        peer = lax.rem(me + step, count)
        push(
            residual.at[me], residual.at[me], r_send_sem.at[peer], r_recv_sem.at[me], "mp", peer
        ).start()
        return carry

    lax.fori_loop(1, count, send_residual, 0)

    def take_residual(step, carry):
        peer = lax.rem(me + count - step, count)
        push(
            residual.at[peer], residual.at[peer], r_send_sem.at[peer], r_recv_sem.at[peer], "mp", peer
        ).wait()
        return carry

    lax.fori_loop(1, count, take_residual, 0)
    squares = jnp.zeros((residual.shape[1], width), F32)
    for chunk in range(count):
        values = residual[chunk].astype(F32)
        squares += values * values
    inverse = lax.rsqrt(jnp.sum(squares, axis=1, keepdims=True) * (1.0 / (count * width)) + EPSILON)
    for chunk in range(count):
        span = pl.ds(chunk * width, width)
        post[:, span] = (residual[chunk].astype(F32) * inverse * gain_ref[:, span]).astype(BF16)
    loads[0].wait()
    gate = jnp.dot(post[...], wg[...], preferred_element_type=F32)
    loads[1].wait()
    up = jnp.dot(post[...], wu[...], preferred_element_type=F32)
    middle = (gate / (1.0 + jnp.exp(-gate)) * up).astype(BF16)
    loads[2].wait()

    def send_down(step, carry):
        peer = lax.rem(me + step, count)
        down_send[peer] = jnp.dot(
            middle, wd[:, columns(peer)], preferred_element_type=F32
        ).astype(BF16)
        push(
            down_send.at[peer], down_recv.at[me], d_send_sem.at[peer], d_recv_sem.at[me], "mp", peer
        ).start()
        return carry

    lax.fori_loop(1, count, send_down, 0)
    total = jnp.dot(middle, wd[:, columns(me)], preferred_element_type=F32)

    def add_down(step, total):
        peer = lax.rem(me + count - step, count)
        push(
            down_send.at[peer], down_recv.at[peer], d_send_sem.at[peer], d_recv_sem.at[peer], "mp", peer
        ).wait()
        return total + down_recv[peer].astype(F32)

    total = lax.fori_loop(1, count, add_down, total)
    out_ref[...] = (residual[me].astype(F32) + total).astype(BF16)


def local(
    hidden_in,
    input_gain,
    w_query,
    key_value_weight,
    query_gain,
    key_gain,
    w_out,
    post_gain,
    w_gate,
    w_up,
    w_down,
    prefix_slot_cache,
    block_table,
    request_prefix,
    suffix_lengths,
):
    seq_count = lax.axis_size("seq")
    model_count = lax.axis_size("mp")
    my_seq = lax.axis_index("seq")
    my_model = lax.axis_index("mp")
    rows, model = hidden_in.shape
    slots, slot_rows, kv_heads, pair_width = prefix_slot_cache.shape
    prefix_length = slots * seq_count // N_PREFIX * slot_rows
    cache_mine = lax.dynamic_slice_in_dim(
        prefix_slot_cache, my_model * kv_heads // model_count, 1, 2
    ).reshape(slots * slot_rows, pair_width)

    positions = my_seq * rows + jnp.arange(rows, dtype=jnp.int32)
    request_ends = jnp.cumsum(suffix_lengths)
    starts = request_ends - suffix_lengths
    inside = (positions[:, None] >= starts[None, :]) & (positions[:, None] < request_ends[None, :])
    start_of = jnp.sum(jnp.where(inside, starts[None, :], 0), axis=1)
    rotary_pos = (prefix_length + positions - start_of).astype(F32)
    half = HEAD // 2
    inverse = jnp.exp(jnp.arange(half).astype(F32) * (-2.0 * math.log(THETA) / HEAD))
    angles = rotary_pos[:, None] * inverse[None, :]
    cosine, sine = jnp.cos(angles), jnp.sin(angles)
    cosine = jnp.concatenate([cosine, cosine], axis=1)
    sine = jnp.concatenate([-sine, sine], axis=1)

    vmem = pl.BlockSpec(memory_space=pltpu.VMEM)
    anywhere = pl.BlockSpec(memory_space=pl.ANY)
    dma = pltpu.SemaphoreType.DMA
    block = jax.ShapeDtypeStruct((rows, HEAD), BF16)
    attended, suffix_key_values = pl.pallas_call(
        functools.partial(attn_kernel, seq_count),
        out_shape=(block, block),
        in_specs=[vmem] * 12,
        out_specs=(vmem, vmem),
        scratch_shapes=[
            pltpu.VMEM((seq_count, rows, HEAD), BF16),
            pltpu.VMEM((slots * slot_rows + rows, HEAD), BF16),
            pltpu.VMEM((HEAD, slots * slot_rows + rows), BF16),
            pltpu.VMEM((seq_count, HEAD, rows), BF16),
            pltpu.VMEM((seq_count, 8, rows), F32),
            pltpu.VMEM((seq_count, HEAD, rows), BF16),
            pltpu.VMEM((seq_count, 8, rows), F32),
        ]
        + [dma((seq_count,))] * 6,
        compiler_params=pltpu.CompilerParams(collective_id=0, has_side_effects=True),
        name="attn",
    )(
        hidden_in,
        input_gain.reshape(1, model),
        w_query,
        key_value_weight,
        query_gain.reshape(1, HEAD),
        key_gain.reshape(1, HEAD),
        cosine,
        sine,
        cache_mine,
        block_table.reshape(1, -1),
        request_prefix.reshape(-1, 1),
        suffix_lengths.reshape(1, -1),
    )
    column_block = (model_count, rows, model // model_count)
    hidden_out = pl.pallas_call(
        functools.partial(ffn_kernel, model_count),
        out_shape=block,
        in_specs=[vmem] * 4 + [anywhere] * 3,
        out_specs=vmem,
        scratch_shapes=[
            pltpu.VMEM(w_gate.shape, BF16),
            pltpu.VMEM(w_up.shape, BF16),
            pltpu.VMEM(w_down.shape, BF16),
            pltpu.VMEM(column_block, BF16),
            pltpu.VMEM(column_block, BF16),
            pltpu.VMEM(column_block, BF16),
            pltpu.VMEM((rows, model), BF16),
            pltpu.VMEM(column_block, BF16),
            pltpu.VMEM(column_block, BF16),
            dma((3,)),
        ]
        + [dma((model_count,))] * 6,
        compiler_params=pltpu.CompilerParams(collective_id=1, has_side_effects=True),
        name="ffn",
    )(
        attended,
        hidden_in,
        w_out,
        post_gain.reshape(1, model),
        w_gate,
        w_up,
        w_down,
    )
    return (hidden_out, suffix_key_values)


def solution(mesh):
    in_specs = (
        P("seq", None),
        P(),
        P(None, "mp"),
        P(None, "mp"),
        P(),
        P(),
        P("mp", None),
        P(),
        P(None, "mp"),
        P(None, "mp"),
        P("mp", None),
        P("seq", None, None, None),
        P(),
        P(),
        P(),
    )
    out_specs = (P("seq", "mp"), P("seq", "mp"))
    return jax.shard_map(local, mesh=mesh, in_specs=in_specs, out_specs=out_specs, check_vma=False)
```

time: 404 us -> 93.7 us (0.23)
  the two profiles are of different devices: /device:TPU:8 before, /device:TPU:32 now
where the time goes in v1:
time: 93.7 us; the launch traced here: 93.4 us
  Pallas kernels  85.7 us (91%)
  local copies, waits for them, and re-layouts  5.61 us (6%)
  other arithmetic  1.37 us (1%)
    pallas_call x1, Pallas kernels, local(): pl.pallas_call(functools.partial(ffn_kernel, model_count), out_shape=bloc...  47.4 us
    pallas_call x1, Pallas kernels, local(): pl.pallas_call(functools.partial(attn_kernel, seq_count), out_shape=(bloc...  38.3 us
    unnamed x11, local copies, waits for them, and re-layouts  4.28 us

profile of v1, /device:TPU:32, one launch (start us, length us, event | category | flops | bytes accessed | tf_op | source)
XLA Modules:
  0.0 93.4 jit_solution(12504468559823190293)
XLA Ops:
  0.6 0.0 copy-start
  0.6 0.0 copy-start.2
  0.7 0.0 copy-start.3
  0.7 1.5 %copy-done = bf16[2,256,8,256]{3,2,1,0:T(8,128)(2,1)S(1)} copy-done((bf16[2,256,8,256]{3,2,1,0:T(8,128)(2,1)S(1)}, bf16[2,256,8,256]{3,2,1,0:T(8,128)(2,1)}, u32[]{:S(2)}) %copy-start) | copy-done | bytes 2097176
  2.2 0.5 constant_dynamic-slice_fusion
  2.8 0.7 copy.25
  3.5 0.0 copy-done.2
  3.5 0.1 copy.22
  3.6 0.1 reduce-window.8
  3.7 0.1 reduce
  3.8 0.1 select_reduce_fusion
  3.9 0.3 fusion
  4.2 0.8 pad_maximum_fusion
  5.0 0.0 copy-done.3
  5.0 0.7 copy.24.prefix_ref
  5.7 38.3 %attn.1 = (bf16[128,128]{1,0:T(8,128)(2,1)}, bf16[128,128]{1,0:T(8,128)(2,1)}) custom-call(bf16[128,2048]{1,0:T(8,128)(2,1)} %hidden_ref.3, f32[1,2048]{1,0:T(1,128)} %bitcast.10, bf16[2048,128]{1,0:T(8,128)(2,1)} %wq_ref.1, bf16[2048,256]{1,0:T(8,128)(2,1)} %wkv_ref.1, f32[1,128]{1,0:T(1,128)} %bitcast.15, f32[1,128]{1,0:T(1,128)} %bitcast.16, ...), custom_call_target="tpu_custom_call" | custom-call | tf_op jit(solution)/shard_map/attn/pallas_call | solution.py:382
  44.0 0.0 copy-start.1
  44.0 47.4 %ffn.1 = bf16[128,128]{1,0:T(8,128)(2,1)} custom-call(bf16[128,128]{1,0:T(8,128)(2,1)} %get-tuple-element.4.att_ref, bf16[128,2048]{1,0:T(8,128)(2,1)} %hidden_ref.3, bf16[128,2048]{1,0:T(8,128)(2,1)} %wo_ref.1, f32[1,2048]{1,0:T(1,128)} %bitcast.11, bf16[2048,384]{1,0:T(8,128)(2,1)} %wg_hbm.1, bf16[2048,384]{1,0:T(8,128)(2,1)} %wu_hbm.1, ...), custom_call_target="tpu_custom_call" | custom-call | tf_op jit(solution)/shard_map/ffn/pallas_call | solution.py:414
  91.5 1.4 %copy.28 = bf16[128,128]{1,0:T(8,128)(2,1)} copy(bf16[128,128]{1,0:T(8,128)(2,1)} %ffn.1) | data formatting | bytes 65536
  92.8 0.0 copy-done.1
  92.8 0.6 copy.29
  (4 shorter events, 0.0 us)
Async XLA Ops:
  0.6 1.6 %copy-start = (bf16[2,256,8,256]{3,2,1,0:T(8,128)(2,1)S(1)}, bf16[2,256,8,256]{3,2,1,0:T(8,128)(2,1)}, u32[]{:S(2)}) copy-start(bf16[2,256,8,256]{3,2,1,0:T(8,128)(2,1)} %param.26) | copy-start | bytes 6291460
  0.6 2.9 %copy-start.2 = (s32[32]{0:T(128)S(1)}, s32[32]{0:T(128)}, u32[]{:S(2)}) copy-start(s32[32]{0:T(128)} %param.29) | copy-start | bytes 388
  0.7 4.3 %copy-start.3 = (s32[32]{0:T(128)S(1)}, s32[32]{0:T(128)}, u32[]{:S(2)}) copy-start(s32[32]{0:T(128)} %param.28) | copy-start | bytes 388
  44.0 48.8 %copy-start.1 = (bf16[128,128]{1,0:T(8,128)(2,1)S(1)}, bf16[128,128]{1,0:T(8,128)(2,1)}, u32[]{:S(2)}) copy-start(bf16[128,128]{1,0:T(8,128)(2,1)} %get-tuple-element.14) | copy-start | bytes 98308
